TPU v7x, 32 devices: a whole 2x2x4 slice. The times are simulated.
32 devices in a mesh: tgt: 8 (over z, core), src: 4 (over y, x).
Axes of the slice: x: 2, y: 2, z: 4, core: 2. Of those that a mesh axis runs over, the one named last changes fastest.
Arguments:
- right_side: float32 [8192], P(('tgt', 'src')), may hold values from -50 to 50
- targets: float32 [3, 8192], P(None, ('tgt', 'src')), may hold values from -1 to 1
- source_nodes: float32 [3, 16, 8192], P(None, None, ('tgt', 'src')), may hold values from -1 to 1
- node_weights: float32 [16, 8192], P(None, ('tgt', 'src')), may hold values from -0.02734375 to 0.02734375
- near_list: int32 [2, 384], P(None, ('tgt', 'src')), may hold values from 0 to 31, as said below
- near_count: int32 [32], P(('tgt', 'src')), may hold values from 1 to 12, as said below
- row_basis: float32 [32, 32, 256], P(('tgt', 'src')), may hold values from -1 to 1
- column_basis: float32 [32, 32, 256], P(('tgt', 'src')), may hold values from -0.375 to 0.375
- coupling: float32 [8, 4, 8, 4, 1024], P('tgt', None, None, 'src'), may hold values from -0.109375 to 0.109375
Outputs:
- solution: float32 [8192], P(('tgt', 'src'))
Inputs may be any that keep to these rules, and one draw needn't show every extreme that they name: `near_list`: for the device with tgt index i and src index j (slots j + i * 4 times 12 onward), every slot names a target cluster c with c // 4 = i and a source cluster d with d % 4 = j; the slots of one device name distinct pairs. `near_count`: some device has all 12 slots live.
All inputs are finite; a program needn't handle non-finite values.
Results may differ from a plain program's by a relative error of at most 0.0003.
Values sent between devices are 32-bit elements; how exact they have to be, the bound alone decides.
No kernel may reach another device: no remote copies, remote signals or barrier semaphores. Data moves between devices by JAX's collectives and lax.ppermute only.
A program may use at most 64 MiB of HBM per device.

v0:
```python
import jax
import jax.numpy as jnp
from jax import lax
from jax.sharding import PartitionSpec as P

spread_sq = 0.0004
norm_floor = 1e-06
highest = lax.Precision.HIGHEST


def tile_values(points, src_nodes, src_weights):
    summed = jnp.zeros((points.shape[1], src_nodes.shape[2]), jnp.float32)
    for node_index in range(src_nodes.shape[1]):
        offset_first = points[0][:, None] - src_nodes[0, node_index][None, :]
        offset_second = points[1][:, None] - src_nodes[1, node_index][None, :]
        offset_third = points[2][:, None] - src_nodes[2, node_index][None, :]
        distance = jnp.sqrt(
            offset_first * offset_first
            + offset_second * offset_second
            + offset_third * offset_third
            + spread_sq
        )
        summed = summed + src_weights[node_index][None, :] / distance
    return summed


def global_sum(value):
    return lax.psum(value, ("tgt", "src"))


def per_device(
    right_side,
    targets,
    source_nodes,
    node_weights,
    near_list,
    near_count,
    row_basis,
    column_basis,
    coupling,
):
    src_count = lax.axis_size("src")
    tgt_count = lax.axis_size("tgt")
    tgt_index = lax.axis_index("tgt")
    leaf_size = right_side.shape[0]
    slot_total = near_list.shape[1]
    rank_size = row_basis.shape[1]
    slot_ids = jnp.arange(slot_total, dtype=jnp.int32)
    live_slot = slot_ids < near_count[0]
    row_local = near_list[0] - tgt_index * src_count
    column_local = near_list[1] // src_count
    row_hits = (
        (row_local[:, None] == jnp.arange(src_count, dtype=jnp.int32)[None, :]) & live_slot[:, None]
    ).astype(jnp.float32)
    column_hits = (column_local[:, None] == jnp.arange(tgt_count, dtype=jnp.int32)[None, :]).astype(
        jnp.float32
    )
    near_mask = jnp.einsum("ka,kb->ab", row_hits, column_hits, precision=highest)
    coupled = (
        coupling.reshape(src_count, tgt_count, rank_size, rank_size)
        * (1.0 - near_mask)[:, :, None, None]
    )
    row_points = lax.all_gather(targets, "src", axis=1, tiled=True)
    row_blocks = row_points.reshape(3, src_count, leaf_size)
    row_bases = lax.all_gather(row_basis, "src", axis=0, tiled=True)
    node_rows, weight_rows = (
        lax.all_gather(source_nodes[None], "tgt", axis=0, tiled=True),
        lax.all_gather(node_weights[None], "tgt", axis=0, tiled=True),
    )

    def make_tile(slot_number):

        def compute(unused):
            return tile_values(
                row_blocks[:, row_local[slot_number]],
                node_rows[column_local[slot_number]],
                weight_rows[column_local[slot_number]],
            )

        def nothing(unused):
            return jnp.zeros((leaf_size, leaf_size), jnp.float32)

        return lax.cond(live_slot[slot_number], compute, nothing, 0)

    tile_cache = lax.map(make_tile, slot_ids)

    def operate(vector):
        coeffs = jnp.dot(column_basis[0], vector, precision=highest)
        value_rows, coeff_rows = (
            lax.all_gather(vector[None], "tgt", axis=0, tiled=True),
            lax.all_gather(coeffs[None], "tgt", axis=0, tiled=True),
        )
        selected = value_rows[column_local]
        contrib = jnp.einsum("kij,kj->ki", tile_cache, selected, precision=highest)
        near_rows = jnp.einsum("ka,ki->ai", row_hits, contrib, precision=highest)
        far_rows = jnp.einsum("abrs,bs->ar", coupled, coeff_rows, precision=highest)
        partial_rows = near_rows + jnp.einsum("ar,arp->ap", far_rows, row_bases, precision=highest)
        own_rows = lax.psum_scatter(partial_rows, "src", scatter_dimension=0, tiled=True)
        result = own_rows[0]
        return 0.5 * vector + result

    rhs_norm = jnp.sqrt(global_sum(jnp.sum(right_side * right_side)) + norm_floor)
    basis_one = right_side / rhs_norm
    image_one = operate(basis_one)
    proj_first = global_sum(jnp.sum(basis_one * image_one))
    rest_one = image_one - proj_first * basis_one
    height_first = jnp.sqrt(global_sum(jnp.sum(rest_one * rest_one)) + norm_floor)
    basis_two = rest_one / height_first
    image_two = operate(basis_two)
    proj_cross = global_sum(jnp.sum(basis_one * image_two))
    rest_two = image_two - proj_cross * basis_one
    proj_second = global_sum(jnp.sum(basis_two * rest_two))
    rest_two = rest_two - proj_second * basis_two
    height_second = jnp.sqrt(global_sum(jnp.sum(rest_two * rest_two)) + norm_floor)
    radius_first = jnp.sqrt(proj_first * proj_first + height_first * height_first)
    cos_first = proj_first / radius_first
    sin_first = height_first / radius_first
    rotated_top = cos_first * proj_cross + sin_first * proj_second
    rotated_low = cos_first * proj_second - sin_first * proj_cross
    radius_second = jnp.sqrt(rotated_low * rotated_low + height_second * height_second)
    coeff_second = -sin_first * rhs_norm * (rotated_low / radius_second) / radius_second
    coeff_first = (cos_first * rhs_norm - rotated_top * coeff_second) / radius_first
    return coeff_first * basis_one + coeff_second * basis_two


def solution(mesh):
    return jax.shard_map(
        per_device,
        mesh=mesh,
        in_specs=(
            P(("tgt", "src")),
            P(None, ("tgt", "src")),
            P(None, None, ("tgt", "src")),
            P(None, ("tgt", "src")),
            P(None, ("tgt", "src")),
            P(("tgt", "src")),
            P(("tgt", "src"), None, None),
            P(("tgt", "src"), None, None),
            P("tgt", None, None, "src", None),
        ),
        out_specs=P(("tgt", "src")),
        check_vma=False,
    )
```

profile of v0, /device:TPU:0, one launch (start us, length us, event | category | flops | bytes accessed | tf_op | source)
XLA Modules:
  0.0 570.9 jit_solution(8423042894770920571)
XLA Ops:
  0.7 0.7 and_select_fusion.1
  1.4 17.0 %all-gather = f32[128,256]{1,0:T(8,128)} all-gather(f32[16,256]{1,0:T(8,128)} %param.16), channel_id=2, replica_groups=mesh['tgt'=8,'src'=4] {'tgt'}, dimensions={0}, use_global_device_ids=true | all-gather | bytes 147456 | tf_op jit(solution)/shard_map/all_gather | solution.py:68
  18.4 0.7 subtract_bitcast_fusion
  19.1 8.3 %all_gather.25 = f32[3,1024]{1,0:T(4,128)S(1)} all-gather(f32[3,256]{1,0:T(4,128)} %param.14), channel_id=1, replica_groups=mesh['tgt'=8,'src'=4] {'src'}, dimensions={1}, use_global_device_ids=true | all-gather | bytes 15360 | tf_op jit(solution)/shard_map/all_gather | solution.py:63
  27.4 15.8 %all-gather.1 = f32[24,16,256]{2,1,0:T(8,128)} all-gather(f32[3,16,256]{2,1,0:T(8,128)} %param.15), channel_id=3, replica_groups=mesh['tgt'=8,'src'=4] {'tgt'}, dimensions={0}, use_global_device_ids=true | all-gather | bytes 442368 | tf_op jit(solution)/shard_map/all_gather | solution.py:67
  43.2 71.8 %while.10 = (s32[]{:T(128)}, f32[12,256,256]{2,1,0:T(8,128)S(1)}, s32[12]{0:T(128)S(1)}, pred[12]{0:T(512)(128)(4,1)S(1)}, s32[12]{0:T(128)S(1)}, /*index=5*/f32...) while((s32[]{:T(128)}, f32[12,256,256]{2,1,0:T(8,128)S(1)}, ...), condition=%wide.region_5.6_spmd, body=%wide.region_2.0_spmd.sunk | while | flops 11468830 | bytes 1091180 | solution.py:85
  47.3 11.1 %conditional.2 = (f32[1,256,256]{2,1,0:T(8,128)S(1)}) conditional(s32[]{:T(128)} %bitcast.164, () %tuple.106, (s32[]{:T(128)}, s32[12]{0:T(128)S(1)}, f32[8,16,256]{2,1,0:T(8,128)}, s32[12]{0:T(128)S(1)}, f32[3,4,256]{2,1,0:T(4,128)S(1)}, /*index=5*/f32[8,3,16,256]{3,2,1,0:T(8,128)}) %tuple.107), branch_computations={%region_3.3_spmd, %region_4.4_spmd} | conditional | flops 11468824 | bytes 566658 | solution.py:83
  51.9 0.8 dynamic-slice_bitcast_fusion
  55.3 1.1 constant_dynamic-slice_fusion.15
  56.5 1.9 multiply_add_fusion
  58.5 0.7 dynamic_slice.26
  62.5 11.1 %conditional.2 = (f32[1,256,256]{2,1,0:T(8,128)S(1)}) conditional(s32[]{:T(128)} %bitcast.164, () %tuple.106, (s32[]{:T(128)}, s32[12]{0:T(128)S(1)}, f32[8,16,256]{2,1,0:T(8,128)}, s32[12]{0:T(128)S(1)}, f32[3,4,256]{2,1,0:T(4,128)S(1)}, /*index=5*/f32[8,3,16,256]{3,2,1,0:T(8,128)}) %tuple.107), branch_computations={%region_3.3_spmd, %region_4.4_spmd} | conditional | flops 11468824 | bytes 566658 | solution.py:83
  67.2 0.8 dynamic-slice_bitcast_fusion
  70.6 1.1 constant_dynamic-slice_fusion.15
  71.7 1.9 multiply_add_fusion
  73.7 0.7 dynamic_slice.26
  77.8 0.7 dynamic_slice.26
  82.0 0.7 dynamic_slice.26
  86.1 0.7 dynamic_slice.26
  90.3 0.7 dynamic_slice.26
  94.4 0.7 dynamic_slice.26
  98.5 0.7 dynamic_slice.26
  102.7 0.7 dynamic_slice.26
  106.8 0.7 dynamic_slice.26
  111.0 0.7 dynamic_slice.26
  115.7 148.6 %psum.42 = f32[]{:T(128)} all-reduce(f32[]{:T(128)} %multiply_reduce_fusion.5), channel_id=1, replica_groups=mesh['tgt'=8,'src'=4] {'tgt','src'}, use_global_device_ids=true, to_apply=%region_1.2 | all-reduce | flops 1 | bytes 8 | tf_op jit(solution)/shard_map/psum | solution.py:28
  265.1 10.7 %all-gather.6 = f32[8,1,256]{2,1,0:T(1,128)S(1)} all-gather(f32[1,1,256]{2,1,0:T(1,128)S(1)} %bitcast.249), channel_id=4, replica_groups=mesh['tgt'=8,'src'=4] {'tgt'}, dimensions={0}, use_global_device_ids=true | all-gather | bytes 9216 | tf_op jit(solution)/shard_map/all_gather | solution.py:90
  276.3 2.7 fusion.12
  280.7 13.9 %all-reduce = f32[256]{0:T(256)S(1)} all-reduce(f32[256]{0:T(256)S(1)} %dynamic-update-slice), channel_id=5, replica_groups=mesh['tgt'=8,'src'=4] {'tgt'}, use_global_device_ids=true, to_apply=%add | all-reduce | flops 256 | bytes 2048
  295.0 1.0 reshape.2740
  296.2 2.2 convolution_bitcast_fusion.1
  298.5 9.4 %all_gather.29 = f32[4,32,256]{2,1,0:T(8,128)S(1)} all-gather(f32[1,32,256]{2,1,0:T(8,128)S(1)} %copy-done.3), channel_id=1, replica_groups=mesh['tgt'=8,'src'=4] {'src'}, dimensions={0}, use_global_device_ids=true | all-gather | bytes 163840 | tf_op jit(solution)/shard_map/all_gather | solution.py:65
  308.3 8.9 %all-reduce.2 = f32[4,256]{1,0:T(4,128)S(1)} all-reduce(f32[4,256]{1,0:T(4,128)S(1)} %convolution_add_fusion.1), channel_id=8, replica_groups=mesh['tgt'=8,'src'=4] {'src'}, use_global_device_ids=true, to_apply=%region_6.7.clone | all-reduce | flops 1024 | bytes 8192
  317.9 0.7 constant_dynamic-slice_fusion.20
  319.2 37.0 %psum.43 = f32[]{:T(128)} all-reduce(f32[]{:T(128)} %multiply_reduce_fusion.4), channel_id=1, replica_groups=mesh['tgt'=8,'src'=4] {'tgt','src'}, use_global_device_ids=true, to_apply=%region_8.9 | all-reduce | flops 1 | bytes 8 | tf_op jit(solution)/shard_map/psum | solution.py:28
  356.2 1.2 multiply_reduce_fusion.3
  357.4 42.4 %psum.44 = f32[]{:T(128)} all-reduce(f32[]{:T(128)} %multiply_reduce_fusion.3), channel_id=1, replica_groups=mesh['tgt'=8,'src'=4] {'tgt','src'}, use_global_device_ids=true, to_apply=%region_10.11 | all-reduce | flops 1 | bytes 8 | tf_op jit(solution)/shard_map/psum | solution.py:28
  402.9 10.2 %all-gather.7 = f32[8,1,256]{2,1,0:T(1,128)S(1)} all-gather(f32[1,1,256]{2,1,0:T(1,128)S(1)} %bitcast.172), channel_id=6, replica_groups=mesh['tgt'=8,'src'=4] {'tgt'}, dimensions={0}, use_global_device_ids=true | all-gather | bytes 9216 | tf_op jit(solution)/shard_map/all_gather | solution.py:90
  413.6 2.7 fusion.10
  416.7 14.0 %all-reduce.1 = f32[256]{0:T(256)S(1)} all-reduce(f32[256]{0:T(256)S(1)} %dynamic-update-slice.1), channel_id=7, replica_groups=mesh['tgt'=8,'src'=4] {'tgt'}, use_global_device_ids=true, to_apply=%add.1 | all-reduce | flops 256 | bytes 2048
  430.8 2.2 convolution_bitcast_fusion
  433.5 10.2 %all-reduce.3 = f32[4,256]{1,0:T(4,128)S(1)} all-reduce(f32[4,256]{1,0:T(4,128)S(1)} %convolution_add_fusion), channel_id=9, replica_groups=mesh['tgt'=8,'src'=4] {'src'}, use_global_device_ids=true, to_apply=%region_11.12.clone | all-reduce | flops 1024 | bytes 8192
  443.7 0.7 constant_dynamic-slice_fusion.19
  445.0 37.0 %psum.45 = f32[]{:T(128)} all-reduce(f32[]{:T(128)} %multiply_reduce_fusion.2), channel_id=1, replica_groups=mesh['tgt'=8,'src'=4] {'tgt','src'}, use_global_device_ids=true, to_apply=%region_13.14 | all-reduce | flops 1 | bytes 8 | tf_op jit(solution)/shard_map/psum | solution.py:28
  482.1 1.3 multiply_reduce_fusion.1
  483.4 42.1 %psum.46 = f32[]{:T(128)} all-reduce(f32[]{:T(128)} %multiply_reduce_fusion.1), channel_id=1, replica_groups=mesh['tgt'=8,'src'=4] {'tgt','src'}, use_global_device_ids=true, to_apply=%region_15.16 | all-reduce | flops 1 | bytes 8 | tf_op jit(solution)/shard_map/psum | solution.py:28
  526.9 1.9 multiply_reduce_fusion
  528.8 39.4 %psum.47 = f32[]{:T(128)} all-reduce(f32[]{:T(128)} %multiply_reduce_fusion), channel_id=1, replica_groups=mesh['tgt'=8,'src'=4] {'tgt','src'}, use_global_device_ids=true, to_apply=%region_17.18 | all-reduce | flops 1 | bytes 8 | tf_op jit(solution)/shard_map/psum | solution.py:28
  (101 shorter events, 20.0 us)
Async XLA Ops:
  0.0 279.1 %copy-start = (f32[1,32,256]{2,1,0:T(8,128)S(1)}, f32[1,32,256]{2,1,0:T(8,128)}, u32[]{:S(2)}) copy-start(f32[1,32,256]{2,1,0:T(8,128)} %param.20) | copy-start | bytes 98308
  43.2 71.9 %copy-start.2 = (f32[256]{0:T(256)S(1)}, f32[256]{0:T(256)}, u32[]{:S(2)}) copy-start(f32[256]{0:T(256)} %param.13) | copy-start | bytes 3076
  43.2 232.5 %copy-start.4 = (s32[2,12]{1,0:T(2,128)S(1)}, s32[2,12]{1,0:T(2,128)}, u32[]{:S(2)}) copy-start(s32[2,12]{1,0:T(2,128)} %param.17) | copy-start | bytes 292
  115.1 164.1 %copy-start.6 = (u32[32]{0:T(128)S(1)}, u32[32]{0:T(128)}, u32[]{:S(2)}) copy-start(u32[32]{0:T(128)} %constant.65) | copy-start | bytes 388
  115.1 179.6 %copy-start.1 = (f32[1,4,8,1,1024]{4,3,2,1,0:T(1,128)S(1)}, f32[1,4,8,1,1024]{4,3,2,1,0:T(1,128)}, u32[]{:S(2)}) copy-start(f32[1,4,8,1,1024]{4,3,2,1,0:T(1,128)} %param.21) | copy-start | bytes 393220
  115.1 183.4 %copy-start.3 = (f32[1,32,256]{2,1,0:T(8,128)S(1)}, f32[1,32,256]{2,1,0:T(8,128)}, u32[]{:S(2)}) copy-start(f32[1,32,256]{2,1,0:T(8,128)} %param.19) | copy-start | bytes 98308
  115.1 202.1 %copy-start.5 = (u32[32]{0:T(128)S(1)}, u32[32]{0:T(128)}, u32[]{:S(2)}) copy-start(u32[32]{0:T(128)} %constant.77) | copy-start | bytes 388
where the time goes:
time: 575 us; the launch traced here: 571 us
  blocking collectives  465 us (81%)
  loops' own time  45.1 us (8%)
  local copies, waits for them, and re-layouts  28.4 us (5%)
  other arithmetic  13 us (2%)
  matrix products  11.4 us (2%)
  between operations  8.12 us (1%)
    psum x6, blocking collectives, global_sum(): return lax.psum(value, ('tgt', 'src'))  346 us
    unnamed x4, blocking collectives  47 us
    another operation x1, loops' own time, per_device(): tile_cache = lax.map(make_tile, slot_ids)  33 us
    all_gather x2, blocking collectives, operate(): lax.all_gather(vector[None], 'tgt', axis=0, tiled=True)  20.8 us
    all_gather x1, blocking collectives, per_device(): lax.all_gather(node_weights[None], 'tgt', axis=0, tiled=True)  17 us
    all_gather x1, blocking collectives, per_device(): lax.all_gather(source_nodes[None], 'tgt', axis=0, tiled=True)  15.8 us
    another operation x12, loops' own time, make_tile(): return lax.cond(live_slot[slot_number], compute, nothing, 0)  12.1 us

commit v1 on v0

v1 whole, which is shorter than its diff:
```python
import functools

import jax
import jax.numpy as jnp
from jax import lax
from jax.experimental import pallas as pl
from jax.experimental.pallas import tpu as pltpu
from jax.sharding import PartitionSpec as P

spread_sq = 0.0004
norm_floor = 1e-06
highest = lax.Precision.HIGHEST
both_axes = ("tgt", "src")
lane_contract = (((1,), (1,)), ((), ()))
plain_contract = (((1,), (0,)), ((), ()))
vmem_space = pl.BlockSpec(memory_space=pltpu.VMEM)
smem_space = pl.BlockSpec(memory_space=pltpu.SMEM)
any_space = pl.BlockSpec(memory_space=pl.ANY)


def in_three(value):
    top = value.astype(jnp.bfloat16)
    rest = value - top.astype(jnp.float32)
    middle = rest.astype(jnp.bfloat16)
    low = (rest - middle.astype(jnp.float32)).astype(jnp.bfloat16)
    return top, middle, low


def exact_dot(value, flags, contract):
    parts = [
        lax.dot_general(part, flags, contract, preferred_element_type=jnp.float32)
        for part in in_three(value)
    ]
    return parts[0] + (parts[1] + parts[2])


def exact_pick(flags, value):
    parts = [
        lax.dot_general(flags, part, plain_contract, preferred_element_type=jnp.float32)
        for part in in_three(value)
    ]
    return parts[0] + (parts[1] + parts[2])


def iota(shape, dim):
    return lax.broadcasted_iota(jnp.int32, shape, dim)


def rows_of(src_count):
    return max(8, src_count)


def pack_kernel(nodes, weights, values, column_basis, packed, *, node_rows):
    packed[...] = jnp.zeros_like(packed)
    for coord in range(3):
        packed[pl.ds(coord * node_rows, node_rows), :] = nodes[coord]
    packed[pl.ds(3 * node_rows, node_rows), :] = weights[...]
    vector = values[...]
    packed[pl.ds(4 * node_rows, 1), :] = vector
    tall = jnp.broadcast_to(vector, (8, vector.shape[1]))
    coeffs = lax.dot_general(
        tall, column_basis[0], lane_contract, precision=highest, preferred_element_type=jnp.float32
    )
    packed[pl.ds(4 * node_rows + 1, 1), pl.ds(0, coeffs.shape[1])] = coeffs[0:1]


def far_rows(coeffs, coupling, keep, row_bases, src_count, tgt_count, rank):
    rows = rows_of(src_count)
    width = coeffs.shape[1]
    spread_flags = (
        (iota((width, rank * rank), 0) % rank) == (iota((width, rank * rank), 1) % rank)
    ).astype(jnp.bfloat16)
    tiled = exact_dot(coeffs, spread_flags, plain_contract)
    row_id = iota((rows, rank * rank), 0) % src_count
    summed = jnp.zeros((rows, rank * rank), jnp.float32)
    for target in range(src_count):
        block = coupling[pl.ds(target * tgt_count, tgt_count), :]
        kept = keep[pl.ds(target * tgt_count, tgt_count), :]
        block = block * jnp.concatenate([kept] * (rank * rank // 128), axis=1)
        total = jnp.sum(block * tiled, axis=0, keepdims=True)
        summed = jnp.where(row_id == target, total, summed)
    stacked = src_count * rank
    group_flags = (
        (iota((stacked, rank * rank), 1) // rank) == (iota((stacked, rank * rank), 0) % rank)
    ).astype(jnp.bfloat16)
    far = exact_dot(summed, group_flags, lane_contract)
    own = (iota((rows, stacked), 1) // rank) == (iota((rows, stacked), 0) % src_count)
    far = jnp.where(own, far, 0.0)
    return lax.dot_general(
        far, row_bases[...], plain_contract, precision=highest, preferred_element_type=jnp.float32
    )


def near_rows(partial, src_count, leaf):
    rows = rows_of(src_count)
    ones = jnp.ones((8, 128), jnp.bfloat16)
    row_id = iota((rows, leaf), 0) % src_count
    result = jnp.zeros((rows, leaf), jnp.float32)
    for target in range(src_count):
        block = partial[target]
        parts = [
            lax.dot_general(ones, part, lane_contract, preferred_element_type=jnp.float32)
            for part in in_three(block)
        ]
        total = (parts[0] + (parts[1] + parts[2]))[0:1]
        result = jnp.where(row_id == target, total, result)
    return result


def clear_partials(partial, keep, src_count):
    keep[...] = jnp.ones_like(keep)
    for target in range(src_count):
        partial[target] = jnp.zeros(partial.shape[1:], jnp.float32)


def add_product(partial, target, start, size, tile, vector):
    half = vector * tile
    total = half[:, 0:128]
    for lane in range(128, tile.shape[1], 128):
        total = total + half[:, lane : lane + 128]
    here = pl.ds(start, size)
    partial[target, here, :] = partial[target, here, :] + total


def first_kernel(
    near_list, near_count, coupling, *refs, src_count, tgt_count, node_rows, rank, leaf
):
    columns = refs[:tgt_count]
    refs = refs[tgt_count:]
    points, refs = refs[:src_count], refs[src_count:]
    rows_in, refs = refs[:src_count], refs[src_count:]
    cols_in, refs = refs[:src_count], refs[src_count:]
    message, tiles_out = refs[:2]
    (held, flat_points, row_bases, col_bases, spread, partial, keep, tiles, far_values) = refs[2:11]
    held_sems, point_sems, row_sems, col_sems, tile_sems = refs[11:]
    tgt_index = lax.axis_index("tgt")
    src_index = lax.axis_index("src")
    copies = []
    for shift in range(src_count):
        there = lax.rem(src_index - shift + src_count, src_count)
        copies.append(
            pltpu.make_async_copy(points[shift], flat_points.at[there], point_sems.at[shift])
        )
    column_copies = []
    for spot in range(tgt_count):
        there = column_place(tgt_index, spot, tgt_count)
        column_copies.append(
            pltpu.make_async_copy(columns[spot], held.at[there], held_sems.at[spot])
        )
    base_copies = []
    for shift in range(src_count):
        there = lax.rem(src_index - shift + src_count, src_count)
        here = pl.ds(pl.multiple_of(there * rank, rank), rank)
        base_copies.append(
            pltpu.make_async_copy(rows_in[shift].at[0], row_bases.at[here, :], row_sems.at[shift])
        )
        base_copies.append(
            pltpu.make_async_copy(cols_in[shift].at[0], col_bases.at[here, :], col_sems.at[shift])
        )
    for copy in copies + column_copies + base_copies:
        copy.start()
    clear_partials(partial, keep, src_count)
    for copy in copies:
        copy.wait()
    for target in range(src_count):
        upright = jnp.transpose(
            jnp.concatenate([flat_points[target], jnp.zeros((5, leaf), jnp.float32)], axis=0)
        )
        for coord in range(3):
            spread[target * 3 + coord] = jnp.broadcast_to(upright[:, coord : coord + 1], (leaf, 128))
    for copy in column_copies:
        copy.wait()
    live = near_count[0]
    block = 32

    def one_slot(slot, carry):
        target = near_list[0, slot] - tgt_index * src_count
        source = near_list[1, slot] // src_count
        keep[pl.ds(target * tgt_count + source, 1), :] = jnp.zeros((1, 128), jnp.float32)

        def one_block(number, inner):
            start = pl.multiple_of(number * block, block)
            here = pl.ds(start, block)
            near = [spread[target * 3 + coord, here, :] for coord in range(3)]
            halves = []
            for lane in range(0, leaf, 128):
                lanes = pl.ds(lane, 128)
                total = None
                for node in range(node_rows):
                    gaps = [
                        near[coord] - held[source, pl.ds(coord * node_rows + node, 1), lanes]
                        for coord in range(3)
                    ]
                    square = gaps[0] * gaps[0] + gaps[1] * gaps[1] + gaps[2] * gaps[2] + spread_sq
                    term = held[source, pl.ds(3 * node_rows + node, 1), lanes] * lax.rsqrt(square)
                    total = term if total is None else total + term
                halves.append(total)
            tile = jnp.concatenate(halves, axis=1)
            tiles[slot, here, :] = tile
            vector = held[source, pl.ds(4 * node_rows, 1), :]
            add_product(partial, target, start, block, tile, vector)
            return inner

        lax.fori_loop(0, leaf // block, one_block, 0)
        pltpu.make_async_copy(tiles.at[slot], tiles_out.at[slot], tile_sems.at[slot]).start()
        return carry

    lax.fori_loop(0, live, one_slot, 0)
    for spot in range(tgt_count):
        far_values[pl.ds(spot, 1), :] = held[spot, pl.ds(4 * node_rows + 1, 1), pl.ds(0, 128)]
    for copy in base_copies:
        copy.wait()
    near = near_rows(partial, src_count, leaf)
    far = far_rows(far_values[...], coupling, keep, row_bases, src_count, tgt_count, rank)
    total = near + far
    rows = rows_of(src_count)
    stacked = src_count * rank
    coeffs = lax.dot_general(
        total, col_bases[...], lane_contract, precision=highest, preferred_element_type=jnp.float32
    )
    own = (iota((rows, stacked), 1) // rank) == (iota((rows, stacked), 0) % src_count)
    coeffs = jnp.where(own, coeffs, 0.0)
    for start in range(0, src_count * tgt_count, rows):
        message[pl.ds(start, rows), pl.ds(0, leaf)] = total
        message[pl.ds(start, rows), pl.ds(leaf, stacked)] = coeffs

    def finish(slot, carry):
        pltpu.make_async_copy(tiles.at[slot], tiles_out.at[slot], tile_sems.at[slot]).wait()
        return carry

    lax.fori_loop(0, live, finish, 0)


def column_place(tgt_index, spot, tgt_count):
    group = 2 if tgt_count % 2 == 0 else 1
    lines = tgt_count // group
    shift, flip = spot % lines, spot // lines
    line = lax.rem(tgt_index // group - shift + lines, lines)
    return line * group + lax.rem(tgt_index % group + flip, group)


def second_kernel(
    near_list, near_count, coupling, received, values, tiles_in, *refs, src_count, tgt_count, rank, leaf
):
    rows_in, refs = refs[:src_count], refs[src_count:]
    message = refs[0]
    (row_bases, partial, keep, tiles, image, row_sems, tile_sems) = refs[1:]
    tgt_index = lax.axis_index("tgt")
    src_index = lax.axis_index("src")
    live = near_count[0]

    def fetch(slot, carry):
        pltpu.make_async_copy(tiles_in.at[slot], tiles.at[slot], tile_sems.at[slot]).start()
        return carry

    lax.fori_loop(0, live, fetch, 0)
    base_copies = []
    for shift in range(src_count):
        there = lax.rem(src_index - shift + src_count, src_count)
        here = pl.ds(pl.multiple_of(there * rank, rank), rank)
        base_copies.append(
            pltpu.make_async_copy(rows_in[shift].at[0], row_bases.at[here, :], row_sems.at[shift])
        )
    for copy in base_copies:
        copy.start()
    clear_partials(partial, keep, src_count)
    stacked = src_count * rank
    groups = (tgt_count, src_count * tgt_count)
    flags = ((iota(groups, 1) // src_count) == iota(groups, 0)).astype(jnp.bfloat16)
    image[...] = exact_pick(flags, received[...])
    block = 64

    def one_slot(slot, carry):
        target = near_list[0, slot] - tgt_index * src_count
        source = near_list[1, slot] // src_count
        keep[pl.ds(target * tgt_count + source, 1), :] = jnp.zeros((1, 128), jnp.float32)
        pltpu.make_async_copy(tiles_in.at[slot], tiles.at[slot], tile_sems.at[slot]).wait()
        vector = image[pl.ds(source, 1), pl.ds(0, leaf)]
        for start in range(0, leaf, block):
            add_product(partial, target, start, block, tiles[slot, pl.ds(start, block), :], vector)
        return carry

    lax.fori_loop(0, live, one_slot, 0)
    for copy in base_copies:
        copy.wait()
    near = near_rows(partial, src_count, leaf)
    far = far_rows(
        image[:, pl.ds(leaf, stacked)], coupling, keep, row_bases, src_count, tgt_count, rank
    )
    total = near + far
    pieces = [total[target : target + 1] for target in range(src_count)]
    pieces.append(image[pl.ds(tgt_index, 1), pl.ds(0, leaf)])
    pieces.append(values[...])
    for number, piece in enumerate(pieces):
        message[:, pl.ds(number * leaf, leaf)] = jnp.broadcast_to(piece, (message.shape[0], leaf))


def third_kernel(received, result, *, src_count, tgt_count, leaf):
    def inner(left, right):
        return jnp.sum(left * right, axis=0, keepdims=True)

    devices = src_count * tgt_count
    groups = (tgt_count, devices)
    flags = ((iota(groups, 1) // src_count) == iota(groups, 0)).astype(jnp.bfloat16)
    images = exact_pick(flags, received[:, pl.ds(0, src_count * leaf)])
    square = (devices, devices)
    place = (iota(square, 0) % tgt_count) * src_count + iota(square, 0) // tgt_count
    flags = (iota(square, 1) == place).astype(jnp.bfloat16)
    others = exact_pick(flags, received[:, pl.ds(src_count * leaf, 2 * leaf)])
    sums = None
    for target in range(src_count):
        twice = images[:, target * leaf : (target + 1) * leaf]
        mine = slice(target * tgt_count, (target + 1) * tgt_count)
        once = others[mine, :leaf]
        start = others[mine, leaf:]
        pairs = [
            (start, start),
            (start, once),
            (once, once),
            (start, twice),
            (once, twice),
            (twice, twice),
        ]
        products = [inner(left, right) for left, right in pairs]
        sums = products if sums is None else [old + new for old, new in zip(sums, products)]
    g00, g01, g11, g02, g12, g22 = [jnp.sum(value, axis=1, keepdims=True) for value in sums]
    rhs_norm = jnp.sqrt(g00 + norm_floor)
    scale = 1.0 / rhs_norm
    proj_first = scale * scale * (0.5 * g00 + g01)
    left = 0.5 - proj_first
    rest_sq = scale * scale * (left * left * g00 + 2.0 * left * g01 + g11)
    height_first = jnp.sqrt(jnp.maximum(rest_sq, 0.0) + norm_floor)
    c1 = scale / height_first
    c0 = left * c1
    i0 = 0.5 * c0
    i1 = 0.5 * c1 + c0
    i2 = c1
    to_start = i0 * g00 + i1 * g01 + i2 * g02
    to_once = i0 * g01 + i1 * g11 + i2 * g12
    proj_cross = scale * to_start
    proj_second = c0 * to_start + c1 * to_once
    r0 = i0 - proj_cross * scale - proj_second * c0
    r1 = i1 - proj_second * c1
    r2 = i2
    last_sq = (
        r0 * (r0 * g00 + 2.0 * (r1 * g01 + r2 * g02))
        + r1 * (r1 * g11 + 2.0 * r2 * g12)
        + r2 * r2 * g22
    )
    height_second = jnp.sqrt(jnp.maximum(last_sq, 0.0) + norm_floor)
    radius_first = jnp.sqrt(proj_first * proj_first + height_first * height_first)
    cos_first = proj_first / radius_first
    sin_first = height_first / radius_first
    rotated_top = cos_first * proj_cross + sin_first * proj_second
    rotated_low = cos_first * proj_second - sin_first * proj_cross
    radius_second = jnp.sqrt(rotated_low * rotated_low + height_second * height_second)
    coeff_second = -sin_first * rhs_norm * (rotated_low / radius_second) / radius_second
    coeff_first = (cos_first * rhs_norm - rotated_top * coeff_second) / radius_first
    me = lax.axis_index("tgt") * src_count + lax.axis_index("src")
    once = received[pl.ds(me, 1), pl.ds(src_count * leaf, leaf)]
    start = received[pl.ds(me, 1), pl.ds((src_count + 1) * leaf, leaf)]
    result[...] = (coeff_first * scale + coeff_second * c0) * start + (coeff_second * c1) * once


def per_device(
    right_side,
    targets,
    source_nodes,
    node_weights,
    near_list,
    near_count,
    row_basis,
    column_basis,
    coupling,
):
    src_count = lax.axis_size("src")
    tgt_count = lax.axis_size("tgt")
    leaf = right_side.shape[0]
    node_rows = node_weights.shape[0]
    rank = row_basis.shape[1]
    slots = near_list.shape[1]
    stacked = src_count * rank
    device_count = src_count * tgt_count
    values = right_side.reshape(1, leaf)
    couplings = coupling.reshape(src_count * tgt_count, rank * rank)
    packed_rows = -(-(4 * node_rows + 2) // 8) * 8

    packed = pl.pallas_call(
        functools.partial(pack_kernel, node_rows=node_rows),
        out_shape=jax.ShapeDtypeStruct((packed_rows, leaf), jnp.float32),
        in_specs=[vmem_space] * 4,
        out_specs=vmem_space,
        name="pack",
    )(source_nodes, node_weights, values, column_basis)

    group = 2 if tgt_count % 2 == 0 else 1
    lines = tgt_count // group

    def from_line(value, shift):
        pairs = [
            (tgt, ((tgt // group + shift) % lines) * group + tgt % group) for tgt in range(tgt_count)
        ]
        return lax.ppermute(value, "tgt", pairs)

    def from_flip(value):
        return lax.ppermute(value, "tgt", [(tgt, tgt ^ 1) for tgt in range(tgt_count)])

    def from_source(value, shift):
        return lax.ppermute(value, "src", [(src, (src + shift) % src_count) for src in range(src_count)])

    columns = [packed] + [from_line(packed, shift) for shift in range(1, lines)]
    if group == 2:
        columns = columns + [from_flip(value) for value in columns]
    points = [targets] + [from_source(targets, shift) for shift in range(1, src_count)]
    rows_in = [row_basis] + [from_source(row_basis, shift) for shift in range(1, src_count)]
    cols_in = [column_basis] + [from_source(column_basis, shift) for shift in range(1, src_count)]

    sizes = dict(src_count=src_count, tgt_count=tgt_count, rank=rank, leaf=leaf)
    message, tiles = pl.pallas_call(
        functools.partial(first_kernel, node_rows=node_rows, **sizes),
        out_shape=(
            jax.ShapeDtypeStruct((device_count, leaf + stacked), jnp.float32),
            jax.ShapeDtypeStruct((slots, leaf, leaf), jnp.float32),
        ),
        in_specs=[smem_space, smem_space, vmem_space]
        + [any_space] * (tgt_count + 3 * src_count),
        out_specs=(vmem_space, any_space),
        scratch_shapes=[
            pltpu.VMEM((tgt_count, packed_rows, leaf), jnp.float32),
            pltpu.VMEM((src_count, 3, leaf), jnp.float32),
            pltpu.VMEM((stacked, leaf), jnp.float32),
            pltpu.VMEM((stacked, leaf), jnp.float32),
            pltpu.VMEM((src_count * 3, leaf, 128), jnp.float32),
            pltpu.VMEM((src_count, leaf, 128), jnp.float32),
            pltpu.VMEM((src_count * tgt_count, 128), jnp.float32),
            pltpu.VMEM((slots, leaf, leaf), jnp.float32),
            pltpu.VMEM((tgt_count, 128), jnp.float32),
            pltpu.SemaphoreType.DMA((tgt_count,)),
            pltpu.SemaphoreType.DMA((src_count,)),
            pltpu.SemaphoreType.DMA((src_count,)),
            pltpu.SemaphoreType.DMA((src_count,)),
            pltpu.SemaphoreType.DMA((slots,)),
        ],
        name="first",
    )(near_list, near_count, couplings, *columns, *points, *rows_in, *cols_in)

    received = lax.all_to_all(message, both_axes, 0, 0, tiled=True)

    message = pl.pallas_call(
        functools.partial(second_kernel, **sizes),
        out_shape=jax.ShapeDtypeStruct((device_count, (src_count + 2) * leaf), jnp.float32),
        in_specs=[smem_space, smem_space, vmem_space, vmem_space, vmem_space]
        + [any_space] * (1 + src_count),
        out_specs=vmem_space,
        scratch_shapes=[
            pltpu.VMEM((stacked, leaf), jnp.float32),
            pltpu.VMEM((src_count, leaf, 128), jnp.float32),
            pltpu.VMEM((src_count * tgt_count, 128), jnp.float32),
            pltpu.VMEM((slots, leaf, leaf), jnp.float32),
            pltpu.VMEM((tgt_count, leaf + stacked), jnp.float32),
            pltpu.SemaphoreType.DMA((src_count,)),
            pltpu.SemaphoreType.DMA((slots,)),
        ],
        name="second",
    )(near_list, near_count, couplings, received, values, tiles, *rows_in)

    received = lax.all_to_all(message, both_axes, 0, 0, tiled=True)

    result = pl.pallas_call(
        functools.partial(third_kernel, src_count=src_count, tgt_count=tgt_count, leaf=leaf),
        out_shape=jax.ShapeDtypeStruct((1, leaf), jnp.float32),
        in_specs=[vmem_space],
        out_specs=vmem_space,
        name="third",
    )(received)
    return result.reshape(leaf)


def solution(mesh):
    return jax.shard_map(
        per_device,
        mesh=mesh,
        in_specs=(
            P(("tgt", "src")),
            P(None, ("tgt", "src")),
            P(None, None, ("tgt", "src")),
            P(None, ("tgt", "src")),
            P(None, ("tgt", "src")),
            P(("tgt", "src")),
            P(("tgt", "src"), None, None),
            P(("tgt", "src"), None, None),
            P("tgt", None, None, "src", None),
        ),
        out_specs=P(("tgt", "src")),
        check_vma=False,
    )
```

time: 575 us -> 94.5 us (0.16)
  blocking collectives: 465 us -> 41.8 us
  loops' own time: 45.1 us -> 0 us
  local copies, waits for them, and re-layouts: 28.4 us -> 5.46 us
  starting transfers between devices: 0 us -> 20.8 us
  Pallas kernels: 0 us -> 14.2 us
  other arithmetic: 13 us -> 0 us
  waiting for transfers between devices: 0 us -> 12.8 us
  matrix products: 11.4 us -> 0 us
  between operations: 8.12 us -> 0.84 us
    psum x6 -> x0, blocking collectives: 346 us -> none  [global_sum(): return lax.psum(value, ('tgt', 'src'))]
    all_gather x6 -> x0, blocking collectives: 71.4 us -> none  [the longest x2 20.8 us: operate(): lax.all_gather(vector[None], 'tgt', axis=0, tiled=True)]
    unnamed x4 -> x0, blocking collectives: 47 us -> none
    another operation x13 -> x0, loops' own time: 45.1 us -> none  [the longest x1 33 us: per_device(): tile_cache = lax.map(make_tile, slot_ids)]
    all_to_all x0 -> x2, blocking collectives: none -> 41.8 us  [per_device(): received = lax.all_to_all(message, both_axes, 0, 0, tiled=True)]
    ppermute x0 -> x16, starting transfers between devices: none -> 20.8 us  [the longest x9 13.7 us: from_source(): lax.ppermute(value, 'src', [(src, (src + shift) % src_count) for src in r...]
    dynamic_slice x28 -> x0, local copies, waits for them, and re-layouts: 18.5 us -> none  [the longest x12 8.02 us: per_device(): tile_cache = lax.map(make_tile, slot_ids)]
    pallas_call x0 -> x4, Pallas kernels: none -> 14.2 us  [the longest x1 6.74 us: per_device(): pl.pallas_call(functools.partial(first_kernel, node_rows=node_rows, **siz...]
  transfers between devices with their start and end apart: 0 -> 16, of which waited for: 0 -> 8; matrix products, arithmetic and copies ran while one was open for 0% -> 2% of each run, Pallas kernels for 0% -> 0%
where the time goes in v1:
time: 94.5 us; the launch traced here: 95.9 us
  blocking collectives  41.8 us (44%)
  starting transfers between devices  20.8 us (22%)
  Pallas kernels  14.2 us (15%)
  waiting for transfers between devices  12.8 us (14%)
  local copies, waits for them, and re-layouts  5.46 us (6%)
    all_to_all x2, blocking collectives, per_device(): received = lax.all_to_all(message, both_axes, 0, 0, tiled=True)  41.8 us
    ppermute x9, starting transfers between devices, from_source(): lax.ppermute(value, 'src', [(src, (src + shift) % src_count) for src in r...  13.7 us
    ppermute x9, waiting for transfers between devices, from_source(): lax.ppermute(value, 'src', [(src, (src + shift) % src_count) for src in r...  12.8 us
    pallas_call x1, Pallas kernels, per_device(): pl.pallas_call(functools.partial(first_kernel, node_rows=node_rows, **siz...  6.74 us
    ppermute x3, starting transfers between devices, from_line(): return lax.ppermute(value, 'tgt', pairs)  6.09 us
    pallas_call x1, Pallas kernels, per_device(): pl.pallas_call(functools.partial(second_kernel, **sizes), out_shape=jax.S...  3.99 us
    unnamed x35, local copies, waits for them, and re-layouts  3.48 us
    all_to_all x2, local copies, waits for them, and re-layouts, per_device(): received = lax.all_to_all(message, both_axes, 0, 0, tiled=True)  1.98 us
  transfers between devices with their start and end apart: 16, of which 8 were waited for; matrix products, arithmetic and copies ran while one was open for 2% of the time, Pallas kernels for 0%

profile of v1, /device:TPU:0, one launch (start us, length us, event | category | flops | bytes accessed | tf_op | source)
XLA Modules:
  0.0 95.9 jit_solution(5353512154684932202)
XLA Ops:
  0.0 1.6 %pack.1.refs_0_ = f32[72,256]{1,0:T(8,128)} custom-call(f32[3,16,256]{2,1,0:T(8,128)} %nodes.1, f32[16,256]{1,0:T(8,128)} %weights.1, f32[1,256]{1,0:T(1,128)} %bitcast.19, f32[1,32,256]{2,1,0:T(8,128)} %refs_16_.1), custom_call_target="tpu_custom_call" | custom-call | tf_op jit(solution)/shard_map/pack/pallas_call | solution.py:388
  1.6 5.1 %collective-permute-start.2 = (f32[72,256]{1,0:T(8,128)}, f32[72,256]{1,0:T(8,128)S(1)}, u32[]{:S(2)}, u32[]{:S(2)}) collective-permute-start(f32[72,256]{1,0:T(8,128)} %pack.1.refs_0_), channel_id=1, source_target_pairs={{0,24},{4,28},{8,0},{12,4},{16,8},{20,12},{24,16},{28,20},{1,25},{... | collective-permute-start | bytes 221192 | tf_op jit(solution)/shard_map/ppermute | solution.py:403
  6.7 0.0 collective-permute-start.1
  6.7 1.0 %collective-permute-start = (f32[72,256]{1,0:T(8,128)}, f32[72,256]{1,0:T(8,128)S(1)}, u32[]{:S(2)}, u32[]{:S(2)}) collective-permute-start(f32[72,256]{1,0:T(8,128)} %pack.1.refs_0_), channel_id=1, source_target_pairs={{0,8},{4,12},{8,16},{12,20},{16,24},{20,28},{24,0},{28,4},{1,9},{5... | collective-permute-start | bytes 221192 | tf_op jit(solution)/shard_map/ppermute | solution.py:403
  7.7 1.5 %collective-permute-start.8 = (f32[3,256]{1,0:T(4,128)}, f32[3,256]{1,0:T(4,128)S(1)}, u32[]{:S(2)}, u32[]{:S(2)}) collective-permute-start(f32[3,256]{1,0:T(4,128)} %refs_8_.1), channel_id=1, source_target_pairs={{0,2},{1,3},{2,0},{3,1},{4,6},{5,7},{6,4},{7,5},{8,10},{9,11},{10,... | collective-permute-start | bytes 9224 | tf_op jit(solution)/shard_map/ppermute | solution.py:409
  9.2 1.4 %collective-permute-start.12 = (f32[1,32,256]{2,1,0:T(8,128)}, f32[1,32,256]{2,1,0:T(8,128)S(1)}, u32[]{:S(2)}, u32[]{:S(2)}) collective-permute-start(f32[1,32,256]{2,1,0:T(8,128)} %refs_0_.1), channel_id=1, source_target_pairs={{0,3},{1,0},{2,1},{3,2},{4,7},{5,4},{6,5},{7,6},{8,11},{9,8},{10,9... | collective-permute-start | bytes 98312 | tf_op jit(solution)/shard_map/ppermute | solution.py:409
  10.6 0.9 collective-permute-done.8.refs_10_
  11.5 1.5 %collective-permute-start.7 = (f32[3,256]{1,0:T(4,128)}, f32[3,256]{1,0:T(4,128)S(1)}, u32[]{:S(2)}, u32[]{:S(2)}) collective-permute-start(f32[3,256]{1,0:T(4,128)} %refs_8_.1), channel_id=1, source_target_pairs={{0,1},{1,2},{2,3},{3,0},{4,5},{5,6},{6,7},{7,4},{8,9},{9,10},{10,1... | collective-permute-start | bytes 9224 | tf_op jit(solution)/shard_map/ppermute | solution.py:409
  13.0 3.2 %collective-permute-done.7.refs_9_ = f32[3,256]{1,0:T(4,128)S(1)} collective-permute-done((f32[3,256]{1,0:T(4,128)}, f32[3,256]{1,0:T(4,128)S(1)}, u32[]{:S(2)}, u32[]{:S(2)}) %collective-permute-start.7) | collective-permute-done | bytes 3104 | tf_op jit(solution)/shard_map/ppermute | solution.py:409
  16.2 1.5 %collective-permute-start.9 = (f32[3,256]{1,0:T(4,128)}, f32[3,256]{1,0:T(4,128)S(1)}, u32[]{:S(2)}, u32[]{:S(2)}) collective-permute-start(f32[3,256]{1,0:T(4,128)} %refs_8_.1), channel_id=1, source_target_pairs={{0,3},{1,0},{2,1},{3,2},{4,7},{5,4},{6,5},{7,6},{8,11},{9,8},{10,9... | collective-permute-start | bytes 9224 | tf_op jit(solution)/shard_map/ppermute | solution.py:409
  17.8 2.3 %collective-permute-done.9.refs_11_ = f32[3,256]{1,0:T(4,128)S(1)} collective-permute-done((f32[3,256]{1,0:T(4,128)}, f32[3,256]{1,0:T(4,128)S(1)}, u32[]{:S(2)}, u32[]{:S(2)}) %collective-permute-start.9) | collective-permute-done | bytes 3104 | tf_op jit(solution)/shard_map/ppermute | solution.py:409
  20.0 1.5 %collective-permute-start.11 = (f32[1,32,256]{2,1,0:T(8,128)}, f32[1,32,256]{2,1,0:T(8,128)S(1)}, u32[]{:S(2)}, u32[]{:S(2)}) collective-permute-start(f32[1,32,256]{2,1,0:T(8,128)} %refs_0_.1), channel_id=1, source_target_pairs={{0,2},{1,3},{2,0},{3,1},{4,6},{5,7},{6,4},{7,5},{8,10},{9,11},{10,... | collective-permute-start | bytes 98312 | tf_op jit(solution)/shard_map/ppermute | solution.py:409
  21.6 0.0 collective-permute-done.12.refs_15_.refs_3_
  21.6 1.5 %collective-permute-start.10 = (f32[1,32,256]{2,1,0:T(8,128)}, f32[1,32,256]{2,1,0:T(8,128)S(1)}, u32[]{:S(2)}, u32[]{:S(2)}) collective-permute-start(f32[1,32,256]{2,1,0:T(8,128)} %refs_0_.1), channel_id=1, source_target_pairs={{0,1},{1,2},{2,3},{3,0},{4,5},{5,6},{6,7},{7,4},{8,9},{9,10},{10,1... | collective-permute-start | bytes 98312 | tf_op jit(solution)/shard_map/ppermute | solution.py:409
  23.1 1.1 %collective-permute-done.11.refs_14_.refs_2_ = f32[1,32,256]{2,1,0:T(8,128)S(1)} collective-permute-done((f32[1,32,256]{2,1,0:T(8,128)}, f32[1,32,256]{2,1,0:T(8,128)S(1)}, u32[]{:S(2)}, u32[]{:S(2)}) %collective-permute-start.11) | collective-permute-done | bytes 32800 | tf_op jit(solution)/shard_map/ppermute | solution.py:409
  24.2 1.5 %collective-permute-start.14 = (f32[1,32,256]{2,1,0:T(8,128)}, f32[1,32,256]{2,1,0:T(8,128)S(1)}, u32[]{:S(2)}, u32[]{:S(2)}) collective-permute-start(f32[1,32,256]{2,1,0:T(8,128)} %refs_16_.1), channel_id=1, source_target_pairs={{0,2},{1,3},{2,0},{3,1},{4,6},{5,7},{6,4},{7,5},{8,10},{9,11},{10,... | collective-permute-start | bytes 98312 | tf_op jit(solution)/shard_map/ppermute | solution.py:409
  25.7 0.9 collective-permute-done.10.refs_13_.refs_1_
  26.6 0.0 collective-permute-start.3
  26.6 0.0 collective-permute-done.2.refs_3_
  26.6 0.5 collective-permute-start.6
  27.1 0.0 collective-permute-done.1.refs_2_
  27.1 0.1 collective-permute-start.5
  27.2 0.0 collective-permute-done.refs_1_
  27.2 0.4 collective-permute-start.4
  27.6 0.7 collective-permute-done.14.refs_18_
  28.3 1.5 %collective-permute-start.13 = (f32[1,32,256]{2,1,0:T(8,128)}, f32[1,32,256]{2,1,0:T(8,128)S(1)}, u32[]{:S(2)}, u32[]{:S(2)}) collective-permute-start(f32[1,32,256]{2,1,0:T(8,128)} %refs_16_.1), channel_id=1, source_target_pairs={{0,1},{1,2},{2,3},{3,0},{4,5},{5,6},{6,7},{7,4},{8,9},{9,10},{10,1... | collective-permute-start | bytes 98312 | tf_op jit(solution)/shard_map/ppermute | solution.py:409
  29.8 3.5 %collective-permute-done.13.refs_17_ = f32[1,32,256]{2,1,0:T(8,128)S(1)} collective-permute-done((f32[1,32,256]{2,1,0:T(8,128)}, f32[1,32,256]{2,1,0:T(8,128)S(1)}, u32[]{:S(2)}, u32[]{:S(2)}) %collective-permute-start.13) | collective-permute-done | bytes 32800 | tf_op jit(solution)/shard_map/ppermute | solution.py:409
  33.3 1.6 %collective-permute-start.15 = (f32[1,32,256]{2,1,0:T(8,128)}, f32[1,32,256]{2,1,0:T(8,128)S(1)}, u32[]{:S(2)}, u32[]{:S(2)}) collective-permute-start(f32[1,32,256]{2,1,0:T(8,128)} %refs_16_.1), channel_id=1, source_target_pairs={{0,3},{1,0},{2,1},{3,2},{4,7},{5,4},{6,5},{7,6},{8,11},{9,8},{10,9... | collective-permute-start | bytes 98312 | tf_op jit(solution)/shard_map/ppermute | solution.py:409
  35.6 1.6 %copy.19 = f32[1,4,8,1,1024]{4,2,3,1,0:T(8,128)} copy(f32[1,4,8,1,1024]{4,3,2,1,0:T(1,128)} %param.17) | data formatting | bytes 262144
  37.1 0.3 collective-permute-done.15.refs_19_
  37.5 0.0 collective-permute-done.3.refs_4_
  37.5 0.0 collective-permute-done.6.refs_7_
  37.5 0.0 collective-permute-done.5.refs_6_
  37.5 0.0 collective-permute-done.4.refs_5_
  37.6 0.4 copy-done.12
  38.1 0.0 copy-done.6
  38.1 0.0 copy-done.7
  38.1 0.0 copy-done.8
  38.2 0.0 copy-done.9
  38.2 6.7 %first.1 = (f32[32,384]{1,0:T(8,128)}, f32[12,256,256]{2,1,0:T(8,128)}) custom-call(s32[2,12]{1,0:T(2,128)} %near_list.3, s32[1]{0:T(128)S(6)} %copy.21.near_count, f32[32,1024]{1,0:T(8,128)} %bitcast.13, f32[72,256]{1,0:T(8,128)} %pack.1.refs_0_, f32[72,256]{1,0:T(8,128)} %copy-done.5, f32[72,256]{1,0:T(8,128)} %copy-done.4, f32[72,256]{1,0:T(8,128)} %copy-done.3, ...), custom_call_target="tpu_custom_call" | custom-call | tf_op jit(solution)/shard_map/first/pallas_call | solution.py:419
  44.9 0.9 copy.10
  45.8 30.6 %all_to_all.22 = f32[32,1,384]{2,1,0:T(1,128)S(1)} all-to-all(f32[32,1,384]{2,1,0:T(1,128)S(1)} %copy.10), channel_id=1, replica_groups=mesh['tgt'=8,'src'=4] {'tgt','src'}, dimensions={0} | all-to-all | bytes 98304 | tf_op jit(solution)/shard_map/all_to_all | solution.py:447
  76.4 0.6 copy.20
  77.0 4.0 %second.1 = f32[32,1536]{1,0:T(8,128)} custom-call(s32[2,12]{1,0:T(2,128)} %near_list.3, s32[1]{0:T(128)S(6)} %copy.21.near_count, f32[32,1024]{1,0:T(8,128)} %bitcast.14, f32[32,384]{1,0:T(8,128)} %bitcast.17, f32[1,256]{1,0:T(1,128)} %bitcast.20, f32[12,256,256]{2,1,0:T(8,128)} %get-tuple-element.8.tiles_in, f32[1,32,256]{2,1,0:T(8,128)} %refs_0_.1, ...), custom_call_target="tpu_custom_call" | custom-call | tf_op jit(solution)/shard_map/second/pallas_call | solution.py:449
  81.0 1.1 %copy.11 = f32[32,1,1536]{2,1,0:T(1,128)S(1)} copy(f32[32,1,1536]{2,0,1:T(8,128)} %bitcast.15) | data formatting | bytes 393216 | tf_op jit(solution)/shard_map/all_to_all | solution.py:467
  82.1 11.2 %all_to_all.23 = f32[32,1,1536]{2,1,0:T(1,128)S(1)} all-to-all(f32[32,1,1536]{2,1,0:T(1,128)S(1)} %copy.11), channel_id=1, replica_groups=mesh['tgt'=8,'src'=4] {'tgt','src'}, dimensions={0} | all-to-all | bytes 393216 | tf_op jit(solution)/shard_map/all_to_all | solution.py:467
  93.3 0.7 copy.18
  94.0 1.9 %third.1 = f32[1,256]{1,0:T(1,128)} custom-call(f32[32,1536]{1,0:T(8,128)} %bitcast.16), custom_call_target="tpu_custom_call" | custom-call | tf_op jit(solution)/shard_map/third/pallas_call | solution.py:469
  (27 shorter events, 0.1 us)
Async XLA Ops:
  1.6 25.0 %collective-permute-start.2 = (f32[72,256]{1,0:T(8,128)}, f32[72,256]{1,0:T(8,128)S(1)}, u32[]{:S(2)}, u32[]{:S(2)}) collective-permute-start(f32[72,256]{1,0:T(8,128)} %pack.1.refs_0_), channel_id=1, source_target_pairs={{0,24},{4,28},{8,0},{12,4},{16,8},{20,12},{24,16},{28,20},{1,25},{... | collective-permute-start | bytes 221192 | tf_op jit(solution)/shard_map/ppermute | solution.py:403
  6.7 20.4 %collective-permute-start.1 = (f32[72,256]{1,0:T(8,128)}, f32[72,256]{1,0:T(8,128)S(1)}, u32[]{:S(2)}, u32[]{:S(2)}) collective-permute-start(f32[72,256]{1,0:T(8,128)} %pack.1.refs_0_), channel_id=1, source_target_pairs={{0,16},{4,20},{8,24},{12,28},{16,0},{20,4},{24,8},{28,12},{1,17},{... | collective-permute-start | bytes 221192 | tf_op jit(solution)/shard_map/ppermute | solution.py:403
  6.7 20.5 %collective-permute-start = (f32[72,256]{1,0:T(8,128)}, f32[72,256]{1,0:T(8,128)S(1)}, u32[]{:S(2)}, u32[]{:S(2)}) collective-permute-start(f32[72,256]{1,0:T(8,128)} %pack.1.refs_0_), channel_id=1, source_target_pairs={{0,8},{4,12},{8,16},{12,20},{16,24},{20,28},{24,0},{28,4},{1,9},{5... | collective-permute-start | bytes 221192 | tf_op jit(solution)/shard_map/ppermute | solution.py:403
  7.7 3.8 %collective-permute-start.8 = (f32[3,256]{1,0:T(4,128)}, f32[3,256]{1,0:T(4,128)S(1)}, u32[]{:S(2)}, u32[]{:S(2)}) collective-permute-start(f32[3,256]{1,0:T(4,128)} %refs_8_.1), channel_id=1, source_target_pairs={{0,2},{1,3},{2,0},{3,1},{4,6},{5,7},{6,4},{7,5},{8,10},{9,11},{10,... | collective-permute-start | bytes 9224 | tf_op jit(solution)/shard_map/ppermute | solution.py:409
  9.2 12.4 %collective-permute-start.12 = (f32[1,32,256]{2,1,0:T(8,128)}, f32[1,32,256]{2,1,0:T(8,128)S(1)}, u32[]{:S(2)}, u32[]{:S(2)}) collective-permute-start(f32[1,32,256]{2,1,0:T(8,128)} %refs_0_.1), channel_id=1, source_target_pairs={{0,3},{1,0},{2,1},{3,2},{4,7},{5,4},{6,5},{7,6},{8,11},{9,8},{10,9... | collective-permute-start | bytes 98312 | tf_op jit(solution)/shard_map/ppermute | solution.py:409
  11.5 26.0 %copy-start.13 = (f32[3,256]{1,0:T(4,128)}, f32[3,256]{1,0:T(4,128)S(1)}, u32[]{:S(2)}) copy-start(f32[3,256]{1,0:T(4,128)S(1)} %collective-permute-done.8.refs_10_) | copy-start | bytes 9220
  11.5 4.7 %collective-permute-start.7 = (f32[3,256]{1,0:T(4,128)}, f32[3,256]{1,0:T(4,128)S(1)}, u32[]{:S(2)}, u32[]{:S(2)}) collective-permute-start(f32[3,256]{1,0:T(4,128)} %refs_8_.1), channel_id=1, source_target_pairs={{0,1},{1,2},{2,3},{3,0},{4,5},{5,6},{6,7},{7,4},{8,9},{9,10},{10,1... | collective-permute-start | bytes 9224 | tf_op jit(solution)/shard_map/ppermute | solution.py:409
  16.2 21.3 %copy-start.14 = (f32[3,256]{1,0:T(4,128)}, f32[3,256]{1,0:T(4,128)S(1)}, u32[]{:S(2)}) copy-start(f32[3,256]{1,0:T(4,128)S(1)} %collective-permute-done.7.refs_9_) | copy-start | bytes 9220
  16.2 3.8 %collective-permute-start.9 = (f32[3,256]{1,0:T(4,128)}, f32[3,256]{1,0:T(4,128)S(1)}, u32[]{:S(2)}, u32[]{:S(2)}) collective-permute-start(f32[3,256]{1,0:T(4,128)} %refs_8_.1), channel_id=1, source_target_pairs={{0,3},{1,0},{2,1},{3,2},{4,7},{5,4},{6,5},{7,6},{8,11},{9,8},{10,9... | collective-permute-start | bytes 9224 | tf_op jit(solution)/shard_map/ppermute | solution.py:409
  20.0 17.5 %copy-start.15 = (f32[3,256]{1,0:T(4,128)}, f32[3,256]{1,0:T(4,128)S(1)}, u32[]{:S(2)}) copy-start(f32[3,256]{1,0:T(4,128)S(1)} %collective-permute-done.9.refs_11_) | copy-start | bytes 9220
  20.0 4.1 %collective-permute-start.11 = (f32[1,32,256]{2,1,0:T(8,128)}, f32[1,32,256]{2,1,0:T(8,128)S(1)}, u32[]{:S(2)}, u32[]{:S(2)}) collective-permute-start(f32[1,32,256]{2,1,0:T(8,128)} %refs_0_.1), channel_id=1, source_target_pairs={{0,2},{1,3},{2,0},{3,1},{4,6},{5,7},{6,4},{7,5},{8,10},{9,11},{10,... | collective-permute-start | bytes 98312 | tf_op jit(solution)/shard_map/ppermute | solution.py:409
  21.6 16.0 %copy-start = (f32[1,32,256]{2,1,0:T(8,128)}, f32[1,32,256]{2,1,0:T(8,128)S(1)}, u32[]{:S(2)}) copy-start(f32[1,32,256]{2,1,0:T(8,128)S(1)} %collective-permute-done.12.refs_15_.refs_3_) | copy-start | bytes 98308
  21.6 5.0 %collective-permute-start.10 = (f32[1,32,256]{2,1,0:T(8,128)}, f32[1,32,256]{2,1,0:T(8,128)S(1)}, u32[]{:S(2)}, u32[]{:S(2)}) collective-permute-start(f32[1,32,256]{2,1,0:T(8,128)} %refs_0_.1), channel_id=1, source_target_pairs={{0,1},{1,2},{2,3},{3,0},{4,5},{5,6},{6,7},{7,4},{8,9},{9,10},{10,1... | collective-permute-start | bytes 98312 | tf_op jit(solution)/shard_map/ppermute | solution.py:409
  24.2 13.4 %copy-start.1 = (f32[1,32,256]{2,1,0:T(8,128)}, f32[1,32,256]{2,1,0:T(8,128)S(1)}, u32[]{:S(2)}) copy-start(f32[1,32,256]{2,1,0:T(8,128)S(1)} %collective-permute-done.11.refs_14_.refs_2_) | copy-start | bytes 98308
  24.2 4.1 %collective-permute-start.14 = (f32[1,32,256]{2,1,0:T(8,128)}, f32[1,32,256]{2,1,0:T(8,128)S(1)}, u32[]{:S(2)}, u32[]{:S(2)}) collective-permute-start(f32[1,32,256]{2,1,0:T(8,128)} %refs_16_.1), channel_id=1, source_target_pairs={{0,2},{1,3},{2,0},{3,1},{4,6},{5,7},{6,4},{7,5},{8,10},{9,11},{10,... | collective-permute-start | bytes 98312 | tf_op jit(solution)/shard_map/ppermute | solution.py:409
  26.6 11.0 %copy-start.2 = (f32[1,32,256]{2,1,0:T(8,128)}, f32[1,32,256]{2,1,0:T(8,128)S(1)}, u32[]{:S(2)}) copy-start(f32[1,32,256]{2,1,0:T(8,128)S(1)} %collective-permute-done.10.refs_13_.refs_1_) | copy-start | bytes 98308
  26.6 10.9 %collective-permute-start.3 = (f32[72,256]{1,0:T(8,128)}, f32[72,256]{1,0:T(8,128)S(1)}, u32[]{:S(2)}, u32[]{:S(2)}) collective-permute-start(f32[72,256]{1,0:T(8,128)} %pack.1.refs_0_), channel_id=1, source_target_pairs={{0,4},{4,0},{8,12},{12,8},{16,20},{20,16},{24,28},{28,24},{1,5},{5... | collective-permute-start | bytes 221192 | tf_op jit(solution)/shard_map/ppermute | solution.py:406
  26.6 11.0 %copy-start.3 = (f32[72,256]{1,0:T(8,128)}, f32[72,256]{1,0:T(8,128)S(1)}, u32[]{:S(2)}) copy-start(f32[72,256]{1,0:T(8,128)S(1)} %collective-permute-done.2.refs_3_) | copy-start | bytes 221188
  26.6 10.8 %collective-permute-start.6 = (f32[72,256]{1,0:T(8,128)S(1)}, f32[72,256]{1,0:T(8,128)S(1)}, u32[]{:S(2)}, u32[]{:S(2)}) collective-permute-start(f32[72,256]{1,0:T(8,128)S(1)} %collective-permute-done.2.refs_3_), channel_id=1, source_target_pairs={{0,4},{4,0},{8,12},{12,8},{16,20},{20,16},{24,28},{28,24},{1,5},{5... | collective-permute-start | bytes 221192 | tf_op jit(solution)/shard_map/ppermute | solution.py:406
  27.1 10.5 %copy-start.4 = (f32[72,256]{1,0:T(8,128)}, f32[72,256]{1,0:T(8,128)S(1)}, u32[]{:S(2)}) copy-start(f32[72,256]{1,0:T(8,128)S(1)} %collective-permute-done.1.refs_2_) | copy-start | bytes 221188
  27.1 10.4 %collective-permute-start.5 = (f32[72,256]{1,0:T(8,128)S(1)}, f32[72,256]{1,0:T(8,128)S(1)}, u32[]{:S(2)}, u32[]{:S(2)}) collective-permute-start(f32[72,256]{1,0:T(8,128)S(1)} %collective-permute-done.1.refs_2_), channel_id=1, source_target_pairs={{0,4},{4,0},{8,12},{12,8},{16,20},{20,16},{24,28},{28,24},{1,5},{5... | collective-permute-start | bytes 221192 | tf_op jit(solution)/shard_map/ppermute | solution.py:406
  27.2 10.4 %copy-start.5 = (f32[72,256]{1,0:T(8,128)}, f32[72,256]{1,0:T(8,128)S(1)}, u32[]{:S(2)}) copy-start(f32[72,256]{1,0:T(8,128)S(1)} %collective-permute-done.refs_1_) | copy-start | bytes 221188
  27.2 10.3 %collective-permute-start.4 = (f32[72,256]{1,0:T(8,128)S(1)}, f32[72,256]{1,0:T(8,128)S(1)}, u32[]{:S(2)}, u32[]{:S(2)}) collective-permute-start(f32[72,256]{1,0:T(8,128)S(1)} %collective-permute-done.refs_1_), channel_id=1, source_target_pairs={{0,4},{4,0},{8,12},{12,8},{16,20},{20,16},{24,28},{28,24},{1,5},{5... | collective-permute-start | bytes 221192 | tf_op jit(solution)/shard_map/ppermute | solution.py:406
  28.3 9.3 %copy-start.10 = (f32[1,32,256]{2,1,0:T(8,128)}, f32[1,32,256]{2,1,0:T(8,128)S(1)}, u32[]{:S(2)}) copy-start(f32[1,32,256]{2,1,0:T(8,128)S(1)} %collective-permute-done.14.refs_18_) | copy-start | bytes 98308
  28.3 5.0 %collective-permute-start.13 = (f32[1,32,256]{2,1,0:T(8,128)}, f32[1,32,256]{2,1,0:T(8,128)S(1)}, u32[]{:S(2)}, u32[]{:S(2)}) collective-permute-start(f32[1,32,256]{2,1,0:T(8,128)} %refs_16_.1), channel_id=1, source_target_pairs={{0,1},{1,2},{2,3},{3,0},{4,5},{5,6},{6,7},{7,4},{8,9},{9,10},{10,1... | collective-permute-start | bytes 98312 | tf_op jit(solution)/shard_map/ppermute | solution.py:409
  33.3 4.3 %copy-start.11 = (f32[1,32,256]{2,1,0:T(8,128)}, f32[1,32,256]{2,1,0:T(8,128)S(1)}, u32[]{:S(2)}) copy-start(f32[1,32,256]{2,1,0:T(8,128)S(1)} %collective-permute-done.13.refs_17_) | copy-start | bytes 98308
  33.3 4.1 %collective-permute-start.15 = (f32[1,32,256]{2,1,0:T(8,128)}, f32[1,32,256]{2,1,0:T(8,128)S(1)}, u32[]{:S(2)}, u32[]{:S(2)}) collective-permute-start(f32[1,32,256]{2,1,0:T(8,128)} %refs_16_.1), channel_id=1, source_target_pairs={{0,3},{1,0},{2,1},{3,2},{4,7},{5,4},{6,5},{7,6},{8,11},{9,8},{10,9... | collective-permute-start | bytes 98312 | tf_op jit(solution)/shard_map/ppermute | solution.py:409
  37.5 0.6 copy-start.12
  37.5 0.6 copy-start.6
  37.5 0.7 copy-start.7
  37.5 0.7 copy-start.8
  37.5 0.7 copy-start.9
